TPU v7x, 32 devices: a whole 2x2x4 slice. The times are simulated.
32 devices in a mesh: dom: 8 (over z, y), grp: 4 (over x, core).
Axes of the slice: x: 2, y: 2, z: 4, core: 2. Of those that a mesh axis runs over, the one named last changes fastest.
Arguments:
- profile: bfloat16 [768, 2, 64, 128], P(('dom', 'grp')), may hold values from -6 to 6
- forcing: bfloat16 [768, 2, 128], P(('dom', 'grp')), may hold values from -6 to 6
- height: bfloat16 [768, 128], P(('dom', 'grp')), may hold values from 0.5 to 2
- area: float32 [768, 128], P(('dom', 'grp')), may hold values from 0.5 to 2
- stretch: int32 [768], P(('dom', 'grp')), may hold values from 0 to 3
- face_cell: int32 [768, 128], P(('dom', 'grp')), may hold values from 0 to 127
- match_owner: int32 [8, 4, 24], P(None, 'grp'), may hold values from 0 to 7, as said below
- match_block: int32 [8, 4, 24], P(None, 'grp'), may hold values from 0 to 11
- live_blocks: int32 [32], replicated, may hold values from 6 to 24, as said below
- cell_velocity: bfloat16 [384, 2, 128], P(('dom', 'grp')), may hold values from -6 to 6
Outputs:
- wall_shear: float32 [768, 2, 128], P(('dom', 'grp'))
- wall_force: float32 [384, 2, 128], P(('dom', 'grp'))
Inputs may be any that keep to these rules, and one draw needn't show every extreme that they name: `match_owner`: of the blocks of one device, at most 6 have the same owner, and in every device one owner has exactly 6. The first live_blocks blocks of a device hold faces. Among the devices of one dom index, exactly one has all 24 blocks in use.
All inputs are finite; a program needn't handle non-finite values.
Results may differ from a plain program's by a relative error of at most 0.001.
Values may be sent and summed in bfloat16 or wider, within the bound.
A program may use at most 64 MiB of HBM per device.

v0:
```python
import functools

import jax
import jax.numpy as jnp
from jax import lax
from jax.experimental import pallas as pl
from jax.experimental.pallas import tpu as pltpu
from jax.sharding import PartitionSpec as P

STEPS = 4
VISCOSITY = 0.005
KARMAN = 0.41
TIME_STEP = 2.0
PUSH_GAIN = 0.5
BASE_RATE = 1.5
MESH = pl.DeviceIdType.MESH
F32 = jnp.float32
BF16 = jnp.bfloat16


def kernel(
    doms,
    grps,
    prof_h,
    forc_h,
    height_h,
    area_h,
    stretch_h,
    face_h,
    owner_h,
    target_h,
    live_h,
    cell_h,
    shear_ref,
    force_ref,
    prof,
    forc,
    height,
    area,
    stretch,
    face,
    owner,
    target,
    live,
    table,
    stage,
    u,
    gval,
    fac,
    base,
    quad,
    gap,
    pick,
    cells,
    packed,
    arrived,
    forc32,
    in_sem,
    own_sem,
    cell_send,
    cell_recv,
    force_send,
    force_recv,
):
    blocks, _, points, faces = prof.shape
    rows = cell_h.shape[0]
    me = lax.axis_index("dom")
    mine = lax.axis_index("grp")
    wide = (blocks, faces)

    barrier = pltpu.get_barrier_semaphore()
    for j in range(1, doms):
        pl.semaphore_signal(
            barrier, inc=1, device_id={"dom": lax.rem(me + j, doms)}, device_id_type=MESH
        )
    loads = []
    for i, (src, dst) in enumerate(
        (
            (stretch_h, stretch),
            (height_h, height),
            (owner_h, owner),
            (target_h, target),
            (face_h, face),
            (prof_h, prof),
            (forc_h, forc),
            (area_h, area),
            (live_h, live),
        )
    ):
        loads.append(pltpu.make_async_copy(src, dst, in_sem.at[i]))
        loads[-1].start()
    own = pltpu.make_async_copy(cell_h, table.at[me], own_sem)
    own.start()
    pl.semaphore_wait(barrier, doms - 1)
    cell_copies = []
    for j in range(1, doms):
        cell_copies.append(
            pltpu.make_async_remote_copy(
                src_ref=cell_h,
                dst_ref=table.at[me],
                send_sem=cell_send.at[j],
                recv_sem=cell_recv.at[j],
                device_id={"dom": lax.rem(me + j, doms)},
                device_id_type=MESH,
            )
        )
        cell_copies[-1].start()
    for load in loads:
        load.wait()

    eye = lax.broadcasted_iota(jnp.int32, (blocks, blocks), 0) == lax.broadcasted_iota(
        jnp.int32, (blocks, blocks), 1
    )

    def as_column(row):
        spread = jnp.broadcast_to(row.astype(F32), (blocks, blocks))
        return jnp.sum(jnp.where(eye, spread, 0.0), axis=1, keepdims=True)

    rate = BASE_RATE + as_column(stretch[...])
    tall = height[...].astype(F32)
    step_rate = jnp.broadcast_to(rate / points, wide)
    growth = jnp.exp(step_rate)
    first = (growth - 1.0) / (jnp.exp(jnp.broadcast_to(rate, wide)) - 1.0)
    base_scale = TIME_STEP * VISCOSITY / (first * tall)
    gap_scale = 0.5 * tall * first * (1.0 + growth)
    mid_scale = 1.0 / (growth - 1.0)
    mid_first = 0.5 * (1.0 + growth)

    def grid_level(m, carry):
        level = m.astype(F32)
        shrink = jnp.exp(-step_rate * level)
        base[m] = base_scale * shrink
        ratio = KARMAN * (mid_first - shrink) * mid_scale
        quad[m] = TIME_STEP * ratio * ratio
        gap[m] = gap_scale * jnp.exp(step_rate * (level - 1.0))
        return carry

    lax.fori_loop(0, points, grid_level, 0)

    def widen(b, carry):
        stage[pl.ds(pl.multiple_of(b * 2 * points, 2 * points), 2 * points), :] = (
            prof[b].astype(F32).reshape(2 * points, faces)
        )
        return carry

    lax.fori_loop(0, blocks, widen, 0)

    def turn(k, carry):
        for c in range(2):
            u[k, c] = stage[pl.ds(c * points + k, blocks, stride=2 * points), :]
        return carry

    lax.fori_loop(0, points, turn, 0)

    forc32[...] = forc[...].astype(F32)
    face_now = face[...]
    cell_ids = lax.broadcasted_iota(jnp.int32, (faces, faces), 0)

    for b in range(blocks):
        pick[b] = (cell_ids == face_now[b : b + 1, :]).astype(F32).astype(BF16)

    row_global = owner[me] * rows + 2 * target[me]
    col_global = as_column(row_global).astype(jnp.int32)
    slots = doms * rows
    slot_lane = lax.broadcasted_iota(jnp.int32, (blocks, slots), 1)
    choose = jnp.concatenate(
        [(slot_lane == col_global + c).astype(F32) for c in range(2)], axis=0
    ).astype(BF16)

    own.wait()
    for copy in cell_copies:
        copy.wait()

    held = table[...].astype(F32).reshape(slots, faces).astype(BF16)
    slot_rows = jnp.dot(choose, held, preferred_element_type=F32)
    matching = [
        jnp.take_along_axis(
            slot_rows[c * blocks : (c + 1) * blocks], face_now, axis=1, mode="promise_in_bounds"
        )
        for c in range(2)
    ]
    source = []
    for c in range(2):
        push = forc32[pl.ds(c, blocks, stride=2), :] + matching[c] - u[points - 1, c]
        source.append(TIME_STEP * PUSH_GAIN * push)
        u[points - 1, c] = matching[c]

    def flux(m, low, high):
        d0 = high[0] - low[0]
        d1 = high[1] - low[1]
        square = d0 * d0 + d1 * d1
        root = square * lax.rsqrt(jnp.maximum(square, 1e-37))
        return base[m] + quad[m] * root

    def point(k):
        return (u[k - 1, 0], u[k - 1, 1])

    zero = jnp.zeros(wide, F32)
    half = points // 2

    def eliminate(k, e, g, near, far, here):
        h = gap[k]
        p = h + near * e
        r = 1.0 / (p + far)
        e_new = p * r
        f_new = far * r
        g_new = tuple((h * (here[c] + source[c]) + near * g[c]) * r for c in range(2))
        return e_new, f_new, g_new

    def time_step(_, carry):
        below = point(1)
        low_flux = flux(0, (zero, zero), below)
        low_e, low_g = jnp.ones(wide, F32), (zero, zero)
        above = point(points - 1)
        edge = point(points)
        high_flux = flux(points - 1, above, edge)
        high_e, high_g = jnp.ones(wide, F32), edge
        for i in range(half):
            k = i + 1
            after = point(k + 1)
            next_flux = flux(k, below, after)
            low_e, low_f, low_g = eliminate(k, low_e, low_g, low_flux, next_flux, below)
            if i < half - 1:
                fac[k] = low_f
                for c in range(2):
                    gval[k, c] = low_g[c]
            low_flux, below = next_flux, after
            k = points - 1 - i
            if k > half:
                after = point(k - 1)
                next_flux = flux(k - 1, after, above)
                high_e, high_f, high_g = eliminate(
                    k, high_e, high_g, high_flux, next_flux, above
                )
                if k > half + 1:
                    fac[k] = high_f
                    for c in range(2):
                        gval[k, c] = high_g[c]
                high_flux, above = next_flux, after
        share = 1.0 / (low_e + low_f * high_e)
        down = [(low_g[c] + low_f * high_g[c]) * share for c in range(2)]
        up = [high_g[c] + high_f * down[c] for c in range(2)]
        for c in range(2):
            u[half - 1, c] = down[c]
            u[half, c] = up[c]
        for i in range(1, half):
            k = half - i
            f = fac[k]
            for c in range(2):
                down[c] = gval[k, c] + f * down[c]
                u[k - 1, c] = down[c]
            k = half + 1 + i
            if k < points:
                f = fac[k]
                for c in range(2):
                    up[c] = gval[k, c] + f * up[c]
                    u[k - 1, c] = up[c]
        return carry

    lax.fori_loop(0, STEPS, time_step, 0)

    wall = point(1)
    wall_flux = flux(0, (zero, zero), wall) * (1.0 / TIME_STEP)
    lane = lax.broadcasted_iota(jnp.int32, live.shape, 1)
    own_live = jnp.sum(
        jnp.where(lane == me * grps + mine, live[...], 0).astype(F32), axis=1, keepdims=True
    )
    alive = lax.broadcasted_iota(jnp.int32, wide, 0).astype(F32) < own_live
    size = area[...]
    pieces = []
    for c in range(2):
        shear = jnp.where(alive, wall_flux * wall[c], 0.0)
        shear_ref[pl.ds(c, blocks, stride=2), :] = shear
        pieces.append(shear * size)
    for c in range(2):
        top = pieces[c].astype(BF16).astype(F32)
        cells[pl.ds(c, blocks, stride=8), :] = top
        cells[pl.ds(2 + c, blocks, stride=8), :] = pieces[c] - top
    for c in range(4):
        cells[pl.ds(4 + c, blocks, stride=8), :] = zero
    for b in range(blocks):
        part = cells[pl.ds(8 * b, 8), :].astype(BF16)
        cells[pl.ds(8 * b, 8), :] = lax.dot_general(
            part, pick[b], (((1,), (1,)), ((), ())), preferred_element_type=F32
        )
    slot_row = lax.broadcasted_iota(jnp.int32, (slots, blocks), 0)
    places, terms = [], []
    for c in range(2):
        by_cell = cells[pl.ds(c, blocks, stride=8), :] + cells[pl.ds(2 + c, blocks, stride=8), :]
        place = (slot_row == row_global + c).astype(F32)
        top = by_cell.astype(BF16).astype(F32)
        places += [place, place]
        terms += [top, by_cell - top]
    total = jnp.dot(
        jnp.concatenate(places, axis=1).astype(BF16),
        jnp.concatenate(terms, axis=0).astype(BF16),
        preferred_element_type=F32,
    )
    packed[...] = total.reshape(doms, rows, faces)
    force_copies = []
    for j in range(1, doms):
        peer = lax.rem(me + j, doms)
        force_copies.append(
            pltpu.make_async_remote_copy(
                src_ref=packed.at[peer],
                dst_ref=arrived.at[j],
                send_sem=force_send.at[j],
                recv_sem=force_recv.at[j],
                device_id={"dom": peer},
                device_id_type=MESH,
            )
        )
        force_copies[-1].start()
    result = packed[me]
    for j in range(1, doms):
        force_copies[j - 1].wait_recv()
        result += arrived[j]
    force_ref[...] = result
    for copy in force_copies:
        copy.wait_send()


def emit(shear_ref, force_ref, shear_out, force_out, sem):
    copies = (
        pltpu.make_async_copy(shear_ref, shear_out, sem.at[0]),
        pltpu.make_async_copy(force_ref, force_out, sem.at[1]),
    )
    for copy in copies:
        copy.start()
    for copy in copies:
        copy.wait()


def body(
    doms,
    grps,
    profile,
    forcing,
    height,
    area,
    stretch,
    face_cell,
    match_owner,
    match_block,
    live_blocks,
    cell_velocity,
):
    blocks, _, points, faces = profile.shape
    rows = 2 * cell_velocity.shape[0]
    everything = pl.BlockSpec(memory_space=pltpu.HBM)
    vmem = pl.BlockSpec(memory_space=pltpu.VMEM)
    deep = (points, blocks, faces)
    dma = pltpu.SemaphoreType.DMA
    vmem_bytes = 32 << 20
    args = (
        profile,
        forcing.reshape(2 * blocks, faces),
        height,
        area,
        stretch.reshape(1, blocks),
        face_cell,
        match_owner,
        match_block,
        live_blocks.reshape(1, -1),
        cell_velocity.reshape(rows, faces),
    )
    shear, force = pl.pallas_call(
        functools.partial(kernel, doms, grps),
        out_shape=(
            jax.ShapeDtypeStruct((2 * blocks, faces), F32),
            jax.ShapeDtypeStruct((rows, faces), F32),
        ),
        in_specs=[everything] * len(args),
        out_specs=(vmem, vmem),
        scratch_shapes=[pltpu.VMEM(arg.shape, arg.dtype) for arg in args[:-1]]
        + [
            pltpu.VMEM((doms, rows, faces), BF16),
            pltpu.VMEM((blocks * 2 * points, faces), F32),
            pltpu.VMEM((points, 2, blocks, faces), F32),
            pltpu.VMEM((points, 2, blocks, faces), F32),
            pltpu.VMEM(deep, F32),
            pltpu.VMEM(deep, F32),
            pltpu.VMEM(deep, F32),
            pltpu.VMEM(deep, F32),
            pltpu.VMEM((blocks, faces, faces), BF16),
            pltpu.VMEM((8 * blocks, faces), F32),
            pltpu.VMEM((doms, rows, faces), F32),
            pltpu.VMEM((doms, rows, faces), F32),
            pltpu.VMEM((2 * blocks, faces), F32),
            dma((len(args) - 1,)),
            dma,
            dma((doms,)),
            dma((doms,)),
            dma((doms,)),
            dma((doms,)),
        ],
        compiler_params=pltpu.CompilerParams(
            collective_id=0, has_side_effects=True, vmem_limit_bytes=vmem_bytes
        ),
        name="wall_model",
    )(*[pltpu.with_memory_space_constraint(x, pltpu.HBM) for x in args])
    shear, force = pl.pallas_call(
        emit,
        out_shape=(
            jax.ShapeDtypeStruct(shear.shape, F32),
            jax.ShapeDtypeStruct(force.shape, F32),
        ),
        in_specs=[pl.BlockSpec(memory_space=pl.ANY)] * 2,
        out_specs=(pl.BlockSpec(memory_space=pl.ANY),) * 2,
        scratch_shapes=[dma((2,))],
        compiler_params=pltpu.CompilerParams(vmem_limit_bytes=1 << 20),
        name="emit",
    )(shear, force)
    return (
        shear.reshape(blocks, 2, faces),
        force.reshape(cell_velocity.shape[0], 2, faces),
    )


def solution(mesh):
    in_specs = (
        P(("dom", "grp"), None, None, None),
        P(("dom", "grp"), None, None),
        P(("dom", "grp"), None),
        P(("dom", "grp"), None),
        P(("dom", "grp")),
        P(("dom", "grp"), None),
        P(None, "grp", None),
        P(None, "grp", None),
        P(),
        P(("dom", "grp"), None, None),
    )
    out_specs = (P(("dom", "grp"), None, None), P(("dom", "grp"), None, None))
    step = functools.partial(body, mesh.shape["dom"], mesh.shape["grp"])
    return jax.shard_map(step, mesh=mesh, in_specs=in_specs, out_specs=out_specs, check_vma=False)
```

profile of v0, /device:TPU:0, one launch (start us, length us, event | category | flops | bytes accessed | tf_op | source)
XLA Modules:
  0.0 20.6 jit_solution(15907645907133630200)
XLA Ops:
  0.6 19.4 %wall_model.1 = (f32[48,128]{1,0:T(8,128)S(1)}, f32[24,128]{1,0:T(8,128)S(1)}) custom-call(bf16[24,2,64,128]{3,2,1,0:T(8,128)(2,1)} %prof_h.1, bf16[48,128]{1,0:T(8,128)(2,1)} %bitcast.6, bf16[24,128]{1,0:T(8,128)(2,1)} %height_h.1, f32[24,128]{1,0:T(8,128)} %area_h.1, s32[1,24]{1,0:T(1,128)} %bitcast.8, s32[24,128]{1,0:T(8,128)} %face_h.1, ...), custom_call_target="tpu_custom_call" | custom-call | tf_op jit(solution)/shard_map/wall_model/pallas_call | solution.py:367
  20.0 0.6 %emit.1 = (f32[48,128]{1,0:T(8,128)}, f32[24,128]{1,0:T(8,128)}) custom-call(f32[48,128]{1,0:T(8,128)S(1)} %get-tuple-element.6.shear_ref, f32[24,128]{1,0:T(8,128)S(1)} %get-tuple-element.7.force_ref), custom_call_target="tpu_custom_call" | custom-call | tf_op jit(solution)/shard_map/emit/pallas_call | solution.py:402
where the time goes:
time: 20.8 us; the launch traced here: 20.6 us
  Pallas kernels  20 us (96%)
  between operations  0.64 us (3%)
    pallas_call x1, Pallas kernels, body(): pl.pallas_call(functools.partial(kernel, doms, grps), out_shape=(jax.Shap...  19.4 us
    pallas_call x1, Pallas kernels, body(): pl.pallas_call(emit, out_shape=(jax.ShapeDtypeStruct(shear.shape, F32), j...  0.63 us

commit v1 on v0

v1 whole, which is shorter than its diff:
```python
import functools

import jax
import jax.numpy as jnp
from jax import lax
from jax.experimental import pallas as pl
from jax.experimental.pallas import tpu as pltpu
from jax.sharding import PartitionSpec as P

STEPS = 4
VISCOSITY = 0.005
KARMAN = 0.41
TIME_STEP = 2.0
PUSH_GAIN = 0.5
BASE_RATE = 1.5
MESH = pl.DeviceIdType.MESH
F32 = jnp.float32
BF16 = jnp.bfloat16


def kernel(
    doms,
    grps,
    prof_h,
    forc_h,
    height_h,
    area_h,
    stretch_h,
    face_h,
    owner_h,
    target_h,
    live_h,
    cell_h,
    shear_ref,
    force_ref,
    prof,
    forc,
    height,
    area,
    stretch,
    face,
    owner,
    target,
    live,
    table,
    jump,
    held_f,
    held_r,
    held_t,
    base,
    quad,
    gap,
    last,
    pick,
    place,
    cells,
    packed,
    arrived,
    forc32,
    in_sem,
    own_sem,
    cell_send,
    cell_recv,
    relay_send,
    relay_recv,
    force_send,
    force_recv,
):
    blocks, _, points, faces = prof.shape
    rows = cell_h.shape[0]
    slots = doms * rows
    half = points // 2
    sub = 8
    relay = min(2, doms - 1)
    me = lax.axis_index("dom")
    mine = lax.axis_index("grp")
    wide = (blocks, faces)

    high = (2 * me) // doms
    spot = high * me + (1 - high) * (doms - 1 - me)

    def peer_at(k):
        step = k + (k - spot + doms) // doms
        return high * step + (1 - high) * (doms - 1 - step)

    barrier = pltpu.get_barrier_semaphore()
    for k in range(doms - 1):
        peer = peer_at(k)

        @pl.when((peer != 0) | (me == relay))
        def _():
            pl.semaphore_signal(barrier, inc=1, device_id={"dom": peer}, device_id_type=MESH)

    own = pltpu.make_async_copy(cell_h, table.at[me], own_sem)
    own.start()
    loads = {}
    for i, (name, src, dst) in enumerate(
        (
            ("stretch", stretch_h, stretch),
            ("height", height_h, height),
            ("owner", owner_h, owner),
            ("target", target_h, target),
            ("face", face_h, face),
            ("prof", prof_h, prof),
            ("forc", forc_h, forc),
            ("area", area_h, area),
            ("live", live_h, live),
        )
    ):
        loads[name] = pltpu.make_async_copy(src, dst, in_sem.at[i])
        loads[name].start()

    def cell_copy(slot, peer, send, recv):
        return pltpu.make_async_remote_copy(
            src_ref=table.at[slot],
            dst_ref=table.at[slot],
            send_sem=send,
            recv_sem=recv,
            device_id={"dom": peer},
            device_id_type=MESH,
        )

    def cells_of(count, send, recv):
        return pltpu.make_async_remote_copy(
            src_ref=table.at[pl.ds(0, count)],
            dst_ref=table.at[pl.ds(0, count)],
            send_sem=send,
            recv_sem=recv,
            device_id={"dom": relay},
            device_id_type=MESH,
        )

    pl.semaphore_wait(barrier, 1 + (doms - 2) * ((me + doms - 1) // doms))
    own.wait()

    @pl.when(me == 0)
    def _():
        cell_copy(0, relay, cell_send, relay_recv).start()

    @pl.when(me == relay)
    def _():
        cell_copy(0, 0, relay_send, relay_recv).wait_recv()
        for peer in range(doms - 1, 0, -1):
            if peer != relay:
                cell_copy(0, peer, relay_send, cell_recv).start()

    @pl.when(me != 0)
    def _():
        for k in range(doms - 1):
            cell_copy(me, peer_at(k), cell_send, cell_recv).start()

    eye = lax.broadcasted_iota(jnp.int32, (blocks, blocks), 0) == lax.broadcasted_iota(
        jnp.int32, (blocks, blocks), 1
    )

    def as_column(row):
        spread = jnp.broadcast_to(row.astype(F32), (blocks, blocks))
        return jnp.sum(jnp.where(eye, spread, 0.0), axis=1, keepdims=True)

    depth = sub * half
    tall_rows = sub * (half + 1)
    row_id = lax.broadcasted_iota(jnp.int32, (tall_rows, depth), 0)
    col_id = lax.broadcasted_iota(jnp.int32, (tall_rows, depth), 1)
    shift = row_id // sub - col_id % half
    same = row_id % sub == col_id // half
    turn = jnp.where(
        same, (shift == 0).astype(F32) - (shift == 1).astype(F32), 0.0
    ).astype(BF16)

    loads["stretch"].wait()
    loads["height"].wait()
    rate = BASE_RATE + as_column(stretch[...])
    tall = height[...].astype(F32)
    step_rate = jnp.broadcast_to(rate / points, wide)
    growth = jnp.exp(step_rate)
    decay = 1.0 / growth
    first = (growth - 1.0) / (jnp.exp(jnp.broadcast_to(rate, wide)) - 1.0)
    gap_scale = 0.5 * tall * first * (1.0 + growth)
    base_scale = TIME_STEP * VISCOSITY / (first * tall * gap_scale)
    quad_scale = TIME_STEP**0.5 * KARMAN / ((growth - 1.0) * gap_scale)
    mid_first = 0.5 * (1.0 + growth)

    def grid_levels(start, base_scale, quad_scale):
        chunk = min(8, half)

        def body(i, carry):
            shrink, space = carry
            for j in range(chunk):
                m = start + i * chunk + j
                base[m] = base_scale * (shrink * shrink)
                ratio = quad_scale * ((mid_first - shrink) * shrink)
                quad[m] = ratio * ratio
                gap[m] = space
                shrink = shrink * decay
                space = space * growth
            return shrink, space

        return lambda carry: lax.fori_loop(0, half // chunk, body, carry)

    shrink, space = grid_levels(0, base_scale, quad_scale)((jnp.ones(wide, F32), gap_scale))
    grid_levels(half, base_scale * growth, quad_scale * growth)((shrink, space * decay))

    for name in ("owner", "target", "face"):
        loads[name].wait()
    face_now = face[...]
    cell_ids = lax.broadcasted_iota(jnp.int32, (faces, faces), 0)
    for b in range(blocks):
        pick[b // 2, :, pl.ds(b % 2 * faces, faces)] = (
            (cell_ids == face_now[b : b + 1, :]).astype(F32).astype(BF16)
        )
    own_row = owner[me]
    aim_row = 2 * target[me]
    col_global = as_column(own_row * rows + aim_row).astype(jnp.int32)
    slot_lane = lax.broadcasted_iota(jnp.int32, (blocks, slots), 1)
    choose = jnp.concatenate(
        [(slot_lane == col_global + c).astype(F32) for c in range(2)], axis=0
    ).astype(BF16)
    terms = 4 * blocks
    widen = (
        lax.broadcasted_iota(jnp.int32, (blocks, terms), 1) // 4
        == lax.broadcasted_iota(jnp.int32, (blocks, terms), 0)
    ).astype(F32).astype(BF16)
    own_wide = jnp.dot(own_row.astype(F32).astype(BF16), widen, preferred_element_type=F32)
    aim_wide = jnp.dot(aim_row.astype(F32).astype(BF16), widen, preferred_element_type=F32)
    comp = lax.broadcasted_iota(jnp.int32, (1, terms), 1) % 2
    slot_of = (own_wide * rows + aim_wide).astype(jnp.int32) + comp
    there = (
        lax.broadcasted_iota(jnp.int32, (slots, terms), 0) == slot_of
    ).astype(F32).astype(BF16)
    place[...] = jnp.concatenate([there, there], axis=1)

    loads["prof"].wait()
    for i in range(blocks // sub):
        group = pl.ds(i * sub, sub)
        for c in range(2):
            below = None
            for part in range(2):
                levels = prof[group, c, pl.ds(part * half, half), :].reshape(depth, faces)
                steps = jnp.dot(turn, levels, preferred_element_type=F32)
                for j in range(half):
                    m = part * half + j
                    step = steps[sub * j : sub * (j + 1)]
                    if j == 0 and part:
                        step += below
                    jump[m, c, group] = gap[m, group] * step
                below = steps[depth:tall_rows]
            last[c, group] = below
    loads["forc"].wait()
    forc32[...] = forc[...].astype(F32)
    loads["area"].wait()
    loads["live"].wait()

    @pl.when(me == relay)
    def _():
        cells_of(doms - 2, cell_send, cell_recv).wait_recv()

    @pl.when(me != relay)
    def _():
        cells_of(doms - 1, cell_send, cell_recv).wait_recv()

    held = table[...].astype(F32).reshape(slots, faces).astype(BF16)
    slot_rows = jnp.dot(choose, held, preferred_element_type=F32)
    edge_low, edge_high = [], []
    for c in range(2):
        matching = jnp.take_along_axis(
            slot_rows[c * blocks : (c + 1) * blocks], face_now, axis=1, mode="promise_in_bounds"
        )
        excess = matching + last[c]
        push = forc32[pl.ds(c, blocks, stride=2), :] + excess
        source = TIME_STEP * PUSH_GAIN * push
        edge_low.append(gap[0] * source)
        edge_high.append(gap[points - 1] * source)
        jump[points - 1, c] = jump[points - 1, c] + gap[points - 1] * excess

    def speed(x):
        return 1.0 / lax.rsqrt(x[0] * x[0] + x[1] * x[1])

    def eliminate(m, ratio, carry, ends):
        x = (jump[m, 0], jump[m, 1])
        slip = 1.0 / (base[m] + quad[m] * speed(x))
        if carry is None:
            near = slip
            t = tuple(x[c] + ends[c] for c in range(2))
        else:
            above, h, t = carry
            near = slip + above
            t = tuple(x[c] + h * t[c] for c in range(2))
        f = 1.0 / (near + 1.0)
        h = ratio * f
        return slip, near, f, t, (near * h, h, t)

    def time_step(_, carry):
        low, high = None, None
        for i in range(half):
            m = i
            slip_low, near_low, f_low, t_low, low = eliminate(m, growth, low, edge_low)
            if i < half - 1:
                held_f[m] = f_low
                held_r[m] = slip_low
                for c in range(2):
                    held_t[m, c] = t_low[c]
            m = points - 1 - i
            slip_high, near_high, f_high, t_high, high = eliminate(
                m, decay, high, [-e for e in edge_high]
            )
            if i < half - 1:
                held_f[m] = f_high
                held_r[m] = slip_high
                for c in range(2):
                    held_t[m, c] = t_high[c]
        share = 1.0 / (near_low + near_high * f_high)
        down = [(t_low[c] + f_high * t_high[c]) * share for c in range(2)]
        up = [f_high * (t_high[c] + down[c]) for c in range(2)]
        for c in range(2):
            jump[half - 1, c] = slip_low * down[c]
            jump[half, c] = slip_high * up[c]
        for i in range(half - 2, -1, -1):
            for m, y in ((i, down), (points - 1 - i, up)):
                f, slip = held_f[m], held_r[m]
                for c in range(2):
                    y[c] = f * (held_t[m, c] + y[c])
                    jump[m, c] = slip * y[c]
        return carry

    lax.fori_loop(0, STEPS, time_step, 0)

    wall = (jump[0, 0], jump[0, 1])
    wall_flux = (base[0] + quad[0] * speed(wall)) * (1.0 / TIME_STEP)
    lane = lax.broadcasted_iota(jnp.int32, live.shape, 1)
    own_live = jnp.sum(
        jnp.where(lane == me * grps + mine, live[...], 0).astype(F32), axis=1, keepdims=True
    )
    alive = lax.broadcasted_iota(jnp.int32, wide, 0).astype(F32) < own_live
    size = area[...]
    for c in range(2):
        shear = jnp.where(alive, wall_flux * wall[c], 0.0)
        shear_ref[pl.ds(c, blocks, stride=2), :] = shear
        piece = shear * size
        top = piece.astype(BF16).astype(F32)
        cells[pl.ds(c, blocks, stride=4), :] = top
        cells[pl.ds(2 + c, blocks, stride=4), :] = piece - top
    upper = lax.broadcasted_iota(jnp.int32, (8, faces), 0) < 4
    for p in range(blocks // 2):
        both = cells[pl.ds(8 * p, 8), :]
        pair = jnp.concatenate(
            [jnp.where(upper, both, 0.0), jnp.where(upper, 0.0, both)], axis=1
        ).astype(BF16)
        cells[pl.ds(8 * p, 8), :] = lax.dot_general(
            pair, pick[p], (((1,), (1,)), ((), ())), preferred_element_type=F32
        )
    by_cell = cells[...]
    top = by_cell.astype(BF16)
    low = (by_cell - top.astype(F32)).astype(BF16)
    total = jnp.dot(
        place[...], jnp.concatenate([top, low], axis=0), preferred_element_type=F32
    )
    packed[...] = total.reshape(doms, rows, faces)
    for k in range(doms - 1):
        peer = peer_at(k)
        pltpu.make_async_remote_copy(
            src_ref=packed.at[peer],
            dst_ref=arrived.at[lax.rem(peer - me + doms, doms) - 1],
            send_sem=force_send,
            recv_sem=force_recv,
            device_id={"dom": peer},
            device_id_type=MESH,
        ).start()
    forces = pltpu.make_async_remote_copy(
        src_ref=packed.at[pl.ds(0, doms - 1)],
        dst_ref=arrived,
        send_sem=force_send,
        recv_sem=force_recv,
        device_id={"dom": relay},
        device_id_type=MESH,
    )
    forces.wait_recv()
    result = packed[me]
    for j in range(doms - 1):
        result += arrived[j]
    force_ref[...] = result
    forces.wait_send()

    @pl.when(me == 0)
    def _():
        cells_of(1, cell_send, relay_recv).wait_send()

    @pl.when(me != 0)
    def _():
        cells_of(doms - 1, cell_send, cell_recv).wait_send()

    @pl.when(me == relay)
    def _():
        cells_of(doms - 2, relay_send, cell_recv).wait_send()


def emit(shear_ref, force_ref, shear_out, force_out, sem):
    copies = (
        pltpu.make_async_copy(shear_ref, shear_out, sem.at[0]),
        pltpu.make_async_copy(force_ref, force_out, sem.at[1]),
    )
    for copy in copies:
        copy.start()
    for copy in copies:
        copy.wait()


def body(
    doms,
    grps,
    profile,
    forcing,
    height,
    area,
    stretch,
    face_cell,
    match_owner,
    match_block,
    live_blocks,
    cell_velocity,
):
    blocks, _, points, faces = profile.shape
    rows = 2 * cell_velocity.shape[0]
    everything = pl.BlockSpec(memory_space=pltpu.HBM)
    vmem = pl.BlockSpec(memory_space=pltpu.VMEM)
    deep = (points, blocks, faces)
    dma = pltpu.SemaphoreType.DMA
    vmem_bytes = 32 << 20
    args = (
        profile,
        forcing.reshape(2 * blocks, faces),
        height,
        area,
        stretch.reshape(1, blocks),
        face_cell,
        match_owner,
        match_block,
        live_blocks.reshape(1, -1),
        cell_velocity.reshape(rows, faces),
    )
    shear, force = pl.pallas_call(
        functools.partial(kernel, doms, grps),
        out_shape=(
            jax.ShapeDtypeStruct((2 * blocks, faces), F32),
            jax.ShapeDtypeStruct((rows, faces), F32),
        ),
        in_specs=[everything] * len(args),
        out_specs=(vmem, vmem),
        scratch_shapes=[pltpu.VMEM(arg.shape, arg.dtype) for arg in args[:-1]]
        + [
            pltpu.VMEM((doms, rows, faces), BF16),
            pltpu.VMEM((points, 2, blocks, faces), F32),
            pltpu.VMEM(deep, F32),
            pltpu.VMEM(deep, F32),
            pltpu.VMEM((points, 2, blocks, faces), F32),
            pltpu.VMEM(deep, F32),
            pltpu.VMEM(deep, F32),
            pltpu.VMEM(deep, F32),
            pltpu.VMEM((2, blocks, faces), F32),
            pltpu.VMEM((blocks // 2, faces, 2 * faces), BF16),
            pltpu.VMEM((doms * rows, 8 * blocks), BF16),
            pltpu.VMEM((4 * blocks, faces), F32),
            pltpu.VMEM((doms, rows, faces), F32),
            pltpu.VMEM((doms - 1, rows, faces), F32),
            pltpu.VMEM((2 * blocks, faces), F32),
            dma((len(args) - 1,)),
            dma,
            dma,
            dma,
            dma,
            dma,
            dma,
            dma,
        ],
        compiler_params=pltpu.CompilerParams(
            collective_id=0, has_side_effects=True, vmem_limit_bytes=vmem_bytes
        ),
        name="wall_model",
    )(*[pltpu.with_memory_space_constraint(x, pltpu.HBM) for x in args])
    shear, force = pl.pallas_call(
        emit,
        out_shape=(
            jax.ShapeDtypeStruct(shear.shape, F32),
            jax.ShapeDtypeStruct(force.shape, F32),
        ),
        in_specs=[pl.BlockSpec(memory_space=pl.ANY)] * 2,
        out_specs=(pl.BlockSpec(memory_space=pl.ANY),) * 2,
        scratch_shapes=[dma((2,))],
        compiler_params=pltpu.CompilerParams(vmem_limit_bytes=1 << 20),
        name="emit",
    )(shear, force)
    return (
        shear.reshape(blocks, 2, faces),
        force.reshape(cell_velocity.shape[0], 2, faces),
    )


def solution(mesh):
    in_specs = (
        P(("dom", "grp"), None, None, None),
        P(("dom", "grp"), None, None),
        P(("dom", "grp"), None),
        P(("dom", "grp"), None),
        P(("dom", "grp")),
        P(("dom", "grp"), None),
        P(None, "grp", None),
        P(None, "grp", None),
        P(),
        P(("dom", "grp"), None, None),
    )
    out_specs = (P(("dom", "grp"), None, None), P(("dom", "grp"), None, None))
    step = functools.partial(body, mesh.shape["dom"], mesh.shape["grp"])
    return jax.shard_map(step, mesh=mesh, in_specs=in_specs, out_specs=out_specs, check_vma=False)
```

time: 20.8 us -> 19 us (0.913)
  Pallas kernels: 20 us -> 18.2 us
    pallas_call x1, Pallas kernels: 19.4 us -> 17.5 us  [body(): pl.pallas_call(functools.partial(kernel, doms, grps), out_shape=(jax.Shap...]
where the time goes in v1:
time: 19 us; the launch traced here: 18.8 us
  Pallas kernels  18.2 us (96%)
  between operations  0.64 us (3%)
    pallas_call x1, Pallas kernels, body(): pl.pallas_call(functools.partial(kernel, doms, grps), out_shape=(jax.Shap...  17.5 us
    pallas_call x1, Pallas kernels, body(): pl.pallas_call(emit, out_shape=(jax.ShapeDtypeStruct(shear.shape, F32), j...  0.63 us

profile of v1, /device:TPU:0, one launch (start us, length us, event | category | flops | bytes accessed | tf_op | source)
XLA Modules:
  0.0 18.8 jit_solution(14388687876484392496)
XLA Ops:
  0.6 17.5 %wall_model.1 = (f32[48,128]{1,0:T(8,128)S(1)}, f32[24,128]{1,0:T(8,128)S(1)}) custom-call(bf16[24,2,64,128]{3,2,1,0:T(8,128)(2,1)} %prof_h.1, bf16[48,128]{1,0:T(8,128)(2,1)} %bitcast.6, bf16[24,128]{1,0:T(8,128)(2,1)} %height_h.1, f32[24,128]{1,0:T(8,128)} %area_h.1, s32[1,24]{1,0:T(1,128)} %bitcast.8, s32[24,128]{1,0:T(8,128)} %face_h.1, ...), custom_call_target="tpu_custom_call" | custom-call | tf_op jit(solution)/shard_map/wall_model/pallas_call | solution.py:440
  18.2 0.6 %emit.1 = (f32[48,128]{1,0:T(8,128)}, f32[24,128]{1,0:T(8,128)}) custom-call(f32[48,128]{1,0:T(8,128)S(1)} %get-tuple-element.6.shear_ref, f32[24,128]{1,0:T(8,128)S(1)} %get-tuple-element.7.force_ref), custom_call_target="tpu_custom_call" | custom-call | tf_op jit(solution)/shard_map/emit/pallas_call | solution.py:479

commit v2 on v1

--- a/solution.py
+++ b/solution.py
@@ -46,11 +46,16 @@
     jump,
     held_f,
     held_r,
+    held_s,
     held_t,
+    fore,
+    by_push,
+    by_top,
     base,
     quad,
     gap,
     last,
+    edge,
     pick,
     place,
     cells,
@@ -250,6 +255,64 @@
     loads["area"].wait()
     loads["live"].wait()
 
+    def speed(x):
+        return 1.0 / lax.rsqrt(x[0] * x[0] + x[1] * x[1])
+
+    def slip_of(m, t):
+        return 1.0 / (base[m] + quad[m] * t)
+
+    top_row = points - 1
+    slip = slip_of(0, speed((jump[0, 0], jump[0, 1])))
+    r = 1.0 / (slip + 1.0)
+    rest = slip * r
+    fore[0] = jnp.ones(wide, F32)
+    held_f[0] = r
+    held_r[0] = slip
+    t = [jump[0, 0], jump[0, 1]]
+    w = None
+    for c in range(2):
+        held_t[0, c] = t[c]
+    for m in range(1, top_row):
+        x = (jump[m, 0], jump[m, 1])
+        slip = slip_of(m, speed(x))
+        if m < half:
+            near = slip + growth * rest
+            g = growth * r
+            r = 1.0 / (near + 1.0)
+        else:
+            near = slip + rest
+            g = r
+            r = 1.0 / (near + decay)
+        rest = near * r
+        t = [x[c] + g * t[c] for c in range(2)]
+        w = g if w is None else g * w
+        held_f[m] = r
+        held_r[m] = slip
+        fore[m] = w
+        for c in range(2):
+            held_t[m, c] = t[c]
+    last_rest = rest
+    y, push_part, top_part = None, None, None
+    for m in range(top_row - 1, -1, -1):
+        r, slip = held_f[m], held_r[m]
+        if y is None:
+            y = [r * held_t[m, c] for c in range(2)]
+            push_part = r * fore[m]
+            top_part = r * decay
+            brink, brink_push = y, push_part
+        else:
+            y = [r * (held_t[m, c] + (y[c] if m < half else decay * y[c])) for c in range(2)]
+            push_part = r * (fore[m] + (push_part if m < half else decay * push_part))
+            top_part = r * (top_part if m < half else decay * top_part)
+        for c in range(2):
+            jump[m, c] = slip * y[c]
+        by_push[m] = slip * push_part
+        by_top[m] = slip * top_part
+    edge[0] = last_rest
+    edge[1] = brink_push
+    for c in range(2):
+        edge[2 + c] = brink[c]
+
     @pl.when(me == relay)
     def _():
         cells_of(doms - 2, cell_send, cell_recv).wait_recv()
@@ -260,7 +323,7 @@
 
     held = table[...].astype(F32).reshape(slots, faces).astype(BF16)
     slot_rows = jnp.dot(choose, held, preferred_element_type=F32)
-    edge_low, edge_high = [], []
+    edge_low, edge_high, x_top = [], [], []
     for c in range(2):
         matching = jnp.take_along_axis(
             slot_rows[c * blocks : (c + 1) * blocks], face_now, axis=1, mode="promise_in_bounds"
@@ -269,62 +332,86 @@
         push = forc32[pl.ds(c, blocks, stride=2), :] + excess
         source = TIME_STEP * PUSH_GAIN * push
         edge_low.append(gap[0] * source)
-        edge_high.append(gap[points - 1] * source)
-        jump[points - 1, c] = jump[points - 1, c] + gap[points - 1] * excess
-
-    def speed(x):
-        return 1.0 / lax.rsqrt(x[0] * x[0] + x[1] * x[1])
-
-    def eliminate(m, ratio, carry, ends):
-        x = (jump[m, 0], jump[m, 1])
-        slip = 1.0 / (base[m] + quad[m] * speed(x))
-        if carry is None:
+        edge_high.append(-gap[top_row] * source)
+        x_top.append(jump[top_row, c] + gap[top_row] * excess)
+    slip = slip_of(top_row, speed(x_top))
+    share = 1.0 / (slip + edge[0])
+    y_top = [
+        (x_top[c] + edge_high[c] + edge[2 + c] + edge_low[c] * edge[1]) * share for c in range(2)
+    ]
+    x_top = [slip * y_top[c] for c in range(2)]
+
+    def first_answer(m):
+        if m == top_row:
+            return x_top
+        return [
+            jump[m, c] + edge_low[c] * by_push[m] + y_top[c] * by_top[m] for c in range(2)
+        ]
+
+    def eliminate(m, ratio, state, ends, first):
+        if first:
+            x = first_answer(m)
+            slip = slip_of(m, speed(x))
+        else:
+            x = [jump[m, c] for c in range(2)]
+            slip = slip_of(m, held_r[m])
+        if state is None:
             near = slip
-            t = tuple(x[c] + ends[c] for c in range(2))
+            t = [x[c] + ends[c] for c in range(2)]
         else:
-            above, h, t = carry
+            above, h, t = state
             near = slip + above
-            t = tuple(x[c] + h * t[c] for c in range(2))
+            t = [x[c] + h * t[c] for c in range(2)]
         f = 1.0 / (near + 1.0)
         h = ratio * f
         return slip, near, f, t, (near * h, h, t)
 
-    def time_step(_, carry):
+    def forward(first):
         low, high = None, None
         for i in range(half):
-            m = i
-            slip_low, near_low, f_low, t_low, low = eliminate(m, growth, low, edge_low)
-            if i < half - 1:
-                held_f[m] = f_low
-                held_r[m] = slip_low
-                for c in range(2):
-                    held_t[m, c] = t_low[c]
-            m = points - 1 - i
-            slip_high, near_high, f_high, t_high, high = eliminate(
-                m, decay, high, [-e for e in edge_high]
-            )
-            if i < half - 1:
-                held_f[m] = f_high
-                held_r[m] = slip_high
-                for c in range(2):
-                    held_t[m, c] = t_high[c]
+            for m in (i, top_row - i):
+                if m == i:
+                    slip, near, f, t, low = ends_low = eliminate(m, growth, low, edge_low, first)
+                else:
+                    slip, near, f, t, high = ends_high = eliminate(m, decay, high, edge_high, first)
+                if i < half - 1:
+                    held_f[m] = f
+                    held_s[m] = slip
+                    for c in range(2):
+                        held_t[m, c] = t[c]
+        return ends_low, ends_high
+
+    def settle(m, slip, y):
+        x = [slip * y[c] for c in range(2)]
+        for c in range(2):
+            jump[m, c] = x[c]
+        held_r[m] = speed(x)
+
+    def backward(ends_low, ends_high, final):
+        slip_low, near_low, _, t_low, _ = ends_low
+        slip_high, near_high, f_high, t_high, _ = ends_high
         share = 1.0 / (near_low + near_high * f_high)
         down = [(t_low[c] + f_high * t_high[c]) * share for c in range(2)]
         up = [f_high * (t_high[c] + down[c]) for c in range(2)]
-        for c in range(2):
-            jump[half - 1, c] = slip_low * down[c]
-            jump[half, c] = slip_high * up[c]
+        if not final:
+            settle(half - 1, slip_low, down)
+            settle(half, slip_high, up)
         for i in range(half - 2, -1, -1):
-            for m, y in ((i, down), (points - 1 - i, up)):
-                f, slip = held_f[m], held_r[m]
+            for m, y in ((i, down), (top_row - i, up)):
+                if final and m != i:
+                    continue
+                f = held_f[m]
                 for c in range(2):
                     y[c] = f * (held_t[m, c] + y[c])
-                    jump[m, c] = slip * y[c]
-        return carry
-
-    lax.fori_loop(0, STEPS, time_step, 0)
-
-    wall = (jump[0, 0], jump[0, 1])
+                if not final:
+                    settle(m, held_s[m], y)
+        return down
+
+    for step in range(1, STEPS):
+        ends = forward(step == 1)
+        down = backward(*ends, step == STEPS - 1)
+
+    wall = [held_s[0] * down[c] for c in range(2)]
     wall_flux = (base[0] + quad[0] * speed(wall)) * (1.0 / TIME_STEP)
     lane = lax.broadcasted_iota(jnp.int32, live.shape, 1)
     own_live = jnp.sum(
@@ -451,11 +538,16 @@
             pltpu.VMEM((points, 2, blocks, faces), F32),
             pltpu.VMEM(deep, F32),
             pltpu.VMEM(deep, F32),
+            pltpu.VMEM(deep, F32),
             pltpu.VMEM((points, 2, blocks, faces), F32),
             pltpu.VMEM(deep, F32),
             pltpu.VMEM(deep, F32),
             pltpu.VMEM(deep, F32),
+            pltpu.VMEM(deep, F32),
+            pltpu.VMEM(deep, F32),
+            pltpu.VMEM(deep, F32),
             pltpu.VMEM((2, blocks, faces), F32),
+            pltpu.VMEM((4, blocks, faces), F32),
             pltpu.VMEM((blocks // 2, faces, 2 * faces), BF16),
             pltpu.VMEM((doms * rows, 8 * blocks), BF16),
             pltpu.VMEM((4 * blocks, faces), F32),

time: 19 us -> 18.4 us (0.968)
  Pallas kernels: 18.2 us -> 17.6 us
    pallas_call x1, Pallas kernels: 17.5 us -> 17 us  [body(): pl.pallas_call(functools.partial(kernel, doms, grps), out_shape=(jax.Shap...]
where the time goes in v2:
time: 18.4 us; the launch traced here: 18.2 us
  Pallas kernels  17.6 us (96%)
  between operations  0.64 us (3%)
    pallas_call x1, Pallas kernels, body(): pl.pallas_call(functools.partial(kernel, doms, grps), out_shape=(jax.Shap...  17 us
    pallas_call x1, Pallas kernels, body(): pl.pallas_call(emit, out_shape=(jax.ShapeDtypeStruct(shear.shape, F32), j...  0.63 us

profile of v2, /device:TPU:0, one launch (start us, length us, event | category | flops | bytes accessed | tf_op | source)
XLA Modules:
  0.0 18.2 jit_solution(1441055260099066873)
XLA Ops:
  0.6 17.0 %wall_model.1 = (f32[48,128]{1,0:T(8,128)S(1)}, f32[24,128]{1,0:T(8,128)S(1)}) custom-call(bf16[24,2,64,128]{3,2,1,0:T(8,128)(2,1)} %prof_h.1, bf16[48,128]{1,0:T(8,128)(2,1)} %bitcast.6, bf16[24,128]{1,0:T(8,128)(2,1)} %height_h.1, f32[24,128]{1,0:T(8,128)} %area_h.1, s32[1,24]{1,0:T(1,128)} %bitcast.8, s32[24,128]{1,0:T(8,128)} %face_h.1, ...), custom_call_target="tpu_custom_call" | custom-call | tf_op jit(solution)/shard_map/wall_model/pallas_call | solution.py:527
  17.6 0.6 %emit.1 = (f32[48,128]{1,0:T(8,128)}, f32[24,128]{1,0:T(8,128)}) custom-call(f32[48,128]{1,0:T(8,128)S(1)} %get-tuple-element.6.shear_ref, f32[24,128]{1,0:T(8,128)S(1)} %get-tuple-element.7.force_ref), custom_call_target="tpu_custom_call" | custom-call | tf_op jit(solution)/shard_map/emit/pallas_call | solution.py:571

commit v3 on v2

--- a/solution.py
+++ b/solution.py
@@ -56,6 +56,12 @@
     gap,
     last,
     edge,
+    middle,
+    held,
+    rows_of,
+    owner_s,
+    target_s,
+    row_at,
     pick,
     place,
     cells,
@@ -82,15 +88,18 @@
     wide = (blocks, faces)
 
     high = (2 * me) // doms
-    spot = high * me + (1 - high) * (doms - 1 - me)
+    odd = (1 - high) * (me % 2) if doms % 2 == 0 else 0
+    spot = high * me + (1 - high) * (doms - 1 - me + odd)
 
     def peer_at(k):
         step = k + (k - spot + doms) // doms
-        return high * step + (1 - high) * (doms - 1 - step)
+        peer = high * step + (1 - high) * (doms - 1 - step)
+        return peer + odd * (1 - 2 * (peer % 2))
 
     barrier = pltpu.get_barrier_semaphore()
-    for k in range(doms - 1):
-        peer = peer_at(k)
+    first = doms // 2 - 1
+    for j in list(range(first, doms)) + list(range(1, first)):
+        peer = lax.rem(me + j, doms)
 
         @pl.when((peer != 0) | (me == relay))
         def _():
@@ -110,10 +119,14 @@
             ("forc", forc_h, forc),
             ("area", area_h, area),
             ("live", live_h, live),
+            ("owner_s", owner_h.at[me], owner_s),
+            ("target_s", target_h.at[me], target_s),
         )
     ):
         loads[name] = pltpu.make_async_copy(src, dst, in_sem.at[i])
         loads[name].start()
+
+    peers = [peer_at(k) for k in range(doms - 1)]
 
     def cell_copy(slot, peer, send, recv):
         return pltpu.make_async_remote_copy(
@@ -144,15 +157,17 @@
 
     @pl.when(me == relay)
     def _():
-        cell_copy(0, 0, relay_send, relay_recv).wait_recv()
-        for peer in range(doms - 1, 0, -1):
-            if peer != relay:
+        cell_copy(0, 1, relay_send, relay_recv).wait_recv()
+
+    @pl.when(me != 0)
+    def _():
+        for peer in peers:
+
+            @pl.when((me == relay) & (peer != 0))
+            def _():
                 cell_copy(0, peer, relay_send, cell_recv).start()
 
-    @pl.when(me != 0)
-    def _():
-        for k in range(doms - 1):
-            cell_copy(me, peer_at(k), cell_send, cell_recv).start()
+            cell_copy(me, peer, cell_send, cell_recv).start()
 
     eye = lax.broadcasted_iota(jnp.int32, (blocks, blocks), 0) == lax.broadcasted_iota(
         jnp.int32, (blocks, blocks), 1
@@ -208,18 +223,14 @@
     for name in ("owner", "target", "face"):
         loads[name].wait()
     face_now = face[...]
-    cell_ids = lax.broadcasted_iota(jnp.int32, (faces, faces), 0)
+    face_down = jnp.transpose(face_now.astype(F32))
+    cell_ids = lax.broadcasted_iota(jnp.int32, (faces, faces), 1).astype(F32)
     for b in range(blocks):
-        pick[b // 2, :, pl.ds(b % 2 * faces, faces)] = (
-            (cell_ids == face_now[b : b + 1, :]).astype(F32).astype(BF16)
+        pick[b // 2, pl.ds(b % 2 * faces, faces), :] = (
+            (cell_ids == face_down[:, b : b + 1]).astype(F32).astype(BF16)
         )
     own_row = owner[me]
     aim_row = 2 * target[me]
-    col_global = as_column(own_row * rows + aim_row).astype(jnp.int32)
-    slot_lane = lax.broadcasted_iota(jnp.int32, (blocks, slots), 1)
-    choose = jnp.concatenate(
-        [(slot_lane == col_global + c).astype(F32) for c in range(2)], axis=0
-    ).astype(BF16)
     terms = 4 * blocks
     widen = (
         lax.broadcasted_iota(jnp.int32, (blocks, terms), 1) // 4
@@ -250,6 +261,10 @@
                     jump[m, c, group] = gap[m, group] * step
                 below = steps[depth:tall_rows]
             last[c, group] = below
+    for name in ("owner_s", "target_s"):
+        loads[name].wait()
+    for b in range(blocks):
+        row_at[b] = owner_s[0, b] * rows + 2 * target_s[0, b]
     loads["forc"].wait()
     forc32[...] = forc[...].astype(F32)
     loads["area"].wait()
@@ -321,12 +336,13 @@
     def _():
         cells_of(doms - 1, cell_send, cell_recv).wait_recv()
 
-    held = table[...].astype(F32).reshape(slots, faces).astype(BF16)
-    slot_rows = jnp.dot(choose, held, preferred_element_type=F32)
+    held[...] = table[...].astype(F32).reshape(slots, faces)
+    for b in range(blocks):
+        rows_of[pl.ds(2 * b, 2), :] = held[pl.ds(row_at[b], 2), :]
     edge_low, edge_high, x_top = [], [], []
     for c in range(2):
         matching = jnp.take_along_axis(
-            slot_rows[c * blocks : (c + 1) * blocks], face_now, axis=1, mode="promise_in_bounds"
+            rows_of[pl.ds(c, blocks, stride=2), :], face_now, axis=1, mode="promise_in_bounds"
         )
         excess = matching + last[c]
         push = forc32[pl.ds(c, blocks, stride=2), :] + excess
@@ -371,31 +387,34 @@
         for i in range(half):
             for m in (i, top_row - i):
                 if m == i:
-                    slip, near, f, t, low = ends_low = eliminate(m, growth, low, edge_low, first)
+                    slip, near, f, t, low = eliminate(m, growth, low, edge_low, first)
                 else:
-                    slip, near, f, t, high = ends_high = eliminate(m, decay, high, edge_high, first)
-                if i < half - 1:
-                    held_f[m] = f
-                    held_s[m] = slip
-                    for c in range(2):
-                        held_t[m, c] = t[c]
-        return ends_low, ends_high
-
-    def settle(m, slip, y):
+                    slip, near, f, t, high = eliminate(m, decay, high, edge_high, first)
+                held_f[m] = f
+                held_s[m] = slip
+                for c in range(2):
+                    held_t[m, c] = t[c]
+                if i == half - 1:
+                    middle[m - i] = near
+
+    def settle(m, y):
+        slip = held_s[m]
         x = [slip * y[c] for c in range(2)]
         for c in range(2):
             jump[m, c] = x[c]
         held_r[m] = speed(x)
 
-    def backward(ends_low, ends_high, final):
-        slip_low, near_low, _, t_low, _ = ends_low
-        slip_high, near_high, f_high, t_high, _ = ends_high
-        share = 1.0 / (near_low + near_high * f_high)
-        down = [(t_low[c] + f_high * t_high[c]) * share for c in range(2)]
-        up = [f_high * (t_high[c] + down[c]) for c in range(2)]
+    def backward(final):
+        f_high = held_f[half]
+        share = 1.0 / (middle[0] + middle[1] * f_high)
+        down, up = [], []
+        for c in range(2):
+            t_high = held_t[half, c]
+            down.append((held_t[half - 1, c] + f_high * t_high) * share)
+            up.append(f_high * (t_high + down[c]))
         if not final:
-            settle(half - 1, slip_low, down)
-            settle(half, slip_high, up)
+            settle(half - 1, down)
+            settle(half, up)
         for i in range(half - 2, -1, -1):
             for m, y in ((i, down), (top_row - i, up)):
                 if final and m != i:
@@ -404,12 +423,18 @@
                 for c in range(2):
                     y[c] = f * (held_t[m, c] + y[c])
                 if not final:
-                    settle(m, held_s[m], y)
+                    settle(m, y)
         return down
 
-    for step in range(1, STEPS):
-        ends = forward(step == 1)
-        down = backward(*ends, step == STEPS - 1)
+    forward(True)
+
+    def time_step(_, carry):
+        backward(False)
+        forward(False)
+        return carry
+
+    lax.fori_loop(2, STEPS, time_step, 0)
+    down = backward(True)
 
     wall = [held_s[0] * down[c] for c in range(2)]
     wall_flux = (base[0] + quad[0] * speed(wall)) * (1.0 / TIME_STEP)
@@ -432,9 +457,7 @@
         pair = jnp.concatenate(
             [jnp.where(upper, both, 0.0), jnp.where(upper, 0.0, both)], axis=1
         ).astype(BF16)
-        cells[pl.ds(8 * p, 8), :] = lax.dot_general(
-            pair, pick[p], (((1,), (1,)), ((), ())), preferred_element_type=F32
-        )
+        cells[pl.ds(8 * p, 8), :] = jnp.dot(pair, pick[p], preferred_element_type=F32)
     by_cell = cells[...]
     top = by_cell.astype(BF16)
     low = (by_cell - top.astype(F32)).astype(BF16)
@@ -442,8 +465,7 @@
         place[...], jnp.concatenate([top, low], axis=0), preferred_element_type=F32
     )
     packed[...] = total.reshape(doms, rows, faces)
-    for k in range(doms - 1):
-        peer = peer_at(k)
+    for peer in peers:
         pltpu.make_async_remote_copy(
             src_ref=packed.at[peer],
             dst_ref=arrived.at[lax.rem(peer - me + doms, doms) - 1],
@@ -548,13 +570,19 @@
             pltpu.VMEM(deep, F32),
             pltpu.VMEM((2, blocks, faces), F32),
             pltpu.VMEM((4, blocks, faces), F32),
-            pltpu.VMEM((blocks // 2, faces, 2 * faces), BF16),
+            pltpu.VMEM((2, blocks, faces), F32),
+            pltpu.VMEM((doms * rows, faces), F32),
+            pltpu.VMEM((2 * blocks, faces), F32),
+            pltpu.SMEM((1, blocks), jnp.int32),
+            pltpu.SMEM((1, blocks), jnp.int32),
+            pltpu.SMEM((blocks,), jnp.int32),
+            pltpu.VMEM((blocks // 2, 2 * faces, faces), BF16),
             pltpu.VMEM((doms * rows, 8 * blocks), BF16),
             pltpu.VMEM((4 * blocks, faces), F32),
             pltpu.VMEM((doms, rows, faces), F32),
             pltpu.VMEM((doms - 1, rows, faces), F32),
             pltpu.VMEM((2 * blocks, faces), F32),
-            dma((len(args) - 1,)),
+            dma((len(args) + 1,)),
             dma,
             dma,
             dma,

time: 18.4 us -> 17.5 us (0.951)
  Pallas kernels: 17.6 us -> 16.7 us
    pallas_call x1, Pallas kernels: 17 us -> 16.1 us  [body(): pl.pallas_call(functools.partial(kernel, doms, grps), out_shape=(jax.Shap...]
where the time goes in v3:
time: 17.5 us; the launch traced here: 17.4 us
  Pallas kernels  16.7 us (95%)
  between operations  0.64 us (4%)
    pallas_call x1, Pallas kernels, body(): pl.pallas_call(functools.partial(kernel, doms, grps), out_shape=(jax.Shap...  16.1 us
    pallas_call x1, Pallas kernels, body(): pl.pallas_call(emit, out_shape=(jax.ShapeDtypeStruct(shear.shape, F32), j...  0.63 us

profile of v3, /device:TPU:0, one launch (start us, length us, event | category | flops | bytes accessed | tf_op | source)
XLA Modules:
  0.0 17.4 jit_solution(6002779729384700370)
XLA Ops:
  0.6 16.1 %wall_model.1 = (f32[48,128]{1,0:T(8,128)S(1)}, f32[24,128]{1,0:T(8,128)S(1)}) custom-call(bf16[24,2,64,128]{3,2,1,0:T(8,128)(2,1)} %prof_h.1, bf16[48,128]{1,0:T(8,128)(2,1)} %bitcast.6, bf16[24,128]{1,0:T(8,128)(2,1)} %height_h.1, f32[24,128]{1,0:T(8,128)} %area_h.1, s32[1,24]{1,0:T(1,128)} %bitcast.8, s32[24,128]{1,0:T(8,128)} %face_h.1, ...), custom_call_target="tpu_custom_call" | custom-call | tf_op jit(solution)/shard_map/wall_model/pallas_call | solution.py:549
  16.7 0.6 %emit.1 = (f32[48,128]{1,0:T(8,128)}, f32[24,128]{1,0:T(8,128)}) custom-call(f32[48,128]{1,0:T(8,128)S(1)} %get-tuple-element.6.shear_ref, f32[24,128]{1,0:T(8,128)S(1)} %get-tuple-element.7.force_ref), custom_call_target="tpu_custom_call" | custom-call | tf_op jit(solution)/shard_map/emit/pallas_call | solution.py:599

commit v4 on v3

--- a/solution.py
+++ b/solution.py
@@ -57,19 +57,20 @@
     last,
     edge,
     middle,
+    scale,
     held,
     rows_of,
     owner_s,
     target_s,
     row_at,
+    spot_at,
+    early_out,
     pick,
     place,
     cells,
     packed,
     arrived,
     forc32,
-    in_sem,
-    own_sem,
     cell_send,
     cell_recv,
     relay_send,
@@ -105,27 +106,6 @@
         def _():
             pl.semaphore_signal(barrier, inc=1, device_id={"dom": peer}, device_id_type=MESH)
 
-    own = pltpu.make_async_copy(cell_h, table.at[me], own_sem)
-    own.start()
-    loads = {}
-    for i, (name, src, dst) in enumerate(
-        (
-            ("stretch", stretch_h, stretch),
-            ("height", height_h, height),
-            ("owner", owner_h, owner),
-            ("target", target_h, target),
-            ("face", face_h, face),
-            ("prof", prof_h, prof),
-            ("forc", forc_h, forc),
-            ("area", area_h, area),
-            ("live", live_h, live),
-            ("owner_s", owner_h.at[me], owner_s),
-            ("target_s", target_h.at[me], target_s),
-        )
-    ):
-        loads[name] = pltpu.make_async_copy(src, dst, in_sem.at[i])
-        loads[name].start()
-
     peers = [peer_at(k) for k in range(doms - 1)]
 
     def cell_copy(slot, peer, send, recv):
@@ -148,128 +128,6 @@
             device_id_type=MESH,
         )
 
-    pl.semaphore_wait(barrier, 1 + (doms - 2) * ((me + doms - 1) // doms))
-    own.wait()
-
-    @pl.when(me == 0)
-    def _():
-        cell_copy(0, relay, cell_send, relay_recv).start()
-
-    @pl.when(me == relay)
-    def _():
-        cell_copy(0, 1, relay_send, relay_recv).wait_recv()
-
-    @pl.when(me != 0)
-    def _():
-        for peer in peers:
-
-            @pl.when((me == relay) & (peer != 0))
-            def _():
-                cell_copy(0, peer, relay_send, cell_recv).start()
-
-            cell_copy(me, peer, cell_send, cell_recv).start()
-
-    eye = lax.broadcasted_iota(jnp.int32, (blocks, blocks), 0) == lax.broadcasted_iota(
-        jnp.int32, (blocks, blocks), 1
-    )
-
-    def as_column(row):
-        spread = jnp.broadcast_to(row.astype(F32), (blocks, blocks))
-        return jnp.sum(jnp.where(eye, spread, 0.0), axis=1, keepdims=True)
-
-    depth = sub * half
-    tall_rows = sub * (half + 1)
-    row_id = lax.broadcasted_iota(jnp.int32, (tall_rows, depth), 0)
-    col_id = lax.broadcasted_iota(jnp.int32, (tall_rows, depth), 1)
-    shift = row_id // sub - col_id % half
-    same = row_id % sub == col_id // half
-    turn = jnp.where(
-        same, (shift == 0).astype(F32) - (shift == 1).astype(F32), 0.0
-    ).astype(BF16)
-
-    loads["stretch"].wait()
-    loads["height"].wait()
-    rate = BASE_RATE + as_column(stretch[...])
-    tall = height[...].astype(F32)
-    step_rate = jnp.broadcast_to(rate / points, wide)
-    growth = jnp.exp(step_rate)
-    decay = 1.0 / growth
-    first = (growth - 1.0) / (jnp.exp(jnp.broadcast_to(rate, wide)) - 1.0)
-    gap_scale = 0.5 * tall * first * (1.0 + growth)
-    base_scale = TIME_STEP * VISCOSITY / (first * tall * gap_scale)
-    quad_scale = TIME_STEP**0.5 * KARMAN / ((growth - 1.0) * gap_scale)
-    mid_first = 0.5 * (1.0 + growth)
-
-    def grid_levels(start, base_scale, quad_scale):
-        chunk = min(8, half)
-
-        def body(i, carry):
-            shrink, space = carry
-            for j in range(chunk):
-                m = start + i * chunk + j
-                base[m] = base_scale * (shrink * shrink)
-                ratio = quad_scale * ((mid_first - shrink) * shrink)
-                quad[m] = ratio * ratio
-                gap[m] = space
-                shrink = shrink * decay
-                space = space * growth
-            return shrink, space
-
-        return lambda carry: lax.fori_loop(0, half // chunk, body, carry)
-
-    shrink, space = grid_levels(0, base_scale, quad_scale)((jnp.ones(wide, F32), gap_scale))
-    grid_levels(half, base_scale * growth, quad_scale * growth)((shrink, space * decay))
-
-    for name in ("owner", "target", "face"):
-        loads[name].wait()
-    face_now = face[...]
-    face_down = jnp.transpose(face_now.astype(F32))
-    cell_ids = lax.broadcasted_iota(jnp.int32, (faces, faces), 1).astype(F32)
-    for b in range(blocks):
-        pick[b // 2, pl.ds(b % 2 * faces, faces), :] = (
-            (cell_ids == face_down[:, b : b + 1]).astype(F32).astype(BF16)
-        )
-    own_row = owner[me]
-    aim_row = 2 * target[me]
-    terms = 4 * blocks
-    widen = (
-        lax.broadcasted_iota(jnp.int32, (blocks, terms), 1) // 4
-        == lax.broadcasted_iota(jnp.int32, (blocks, terms), 0)
-    ).astype(F32).astype(BF16)
-    own_wide = jnp.dot(own_row.astype(F32).astype(BF16), widen, preferred_element_type=F32)
-    aim_wide = jnp.dot(aim_row.astype(F32).astype(BF16), widen, preferred_element_type=F32)
-    comp = lax.broadcasted_iota(jnp.int32, (1, terms), 1) % 2
-    slot_of = (own_wide * rows + aim_wide).astype(jnp.int32) + comp
-    there = (
-        lax.broadcasted_iota(jnp.int32, (slots, terms), 0) == slot_of
-    ).astype(F32).astype(BF16)
-    place[...] = jnp.concatenate([there, there], axis=1)
-
-    loads["prof"].wait()
-    for i in range(blocks // sub):
-        group = pl.ds(i * sub, sub)
-        for c in range(2):
-            below = None
-            for part in range(2):
-                levels = prof[group, c, pl.ds(part * half, half), :].reshape(depth, faces)
-                steps = jnp.dot(turn, levels, preferred_element_type=F32)
-                for j in range(half):
-                    m = part * half + j
-                    step = steps[sub * j : sub * (j + 1)]
-                    if j == 0 and part:
-                        step += below
-                    jump[m, c, group] = gap[m, group] * step
-                below = steps[depth:tall_rows]
-            last[c, group] = below
-    for name in ("owner_s", "target_s"):
-        loads[name].wait()
-    for b in range(blocks):
-        row_at[b] = owner_s[0, b] * rows + 2 * target_s[0, b]
-    loads["forc"].wait()
-    forc32[...] = forc[...].astype(F32)
-    loads["area"].wait()
-    loads["live"].wait()
-
     def speed(x):
         return 1.0 / lax.rsqrt(x[0] * x[0] + x[1] * x[1])
 
@@ -277,56 +135,209 @@
         return 1.0 / (base[m] + quad[m] * t)
 
     top_row = points - 1
-    slip = slip_of(0, speed((jump[0, 0], jump[0, 1])))
-    r = 1.0 / (slip + 1.0)
-    rest = slip * r
-    fore[0] = jnp.ones(wide, F32)
-    held_f[0] = r
-    held_r[0] = slip
-    t = [jump[0, 0], jump[0, 1]]
-    w = None
-    for c in range(2):
-        held_t[0, c] = t[c]
-    for m in range(1, top_row):
-        x = (jump[m, 0], jump[m, 1])
-        slip = slip_of(m, speed(x))
-        if m < half:
-            near = slip + growth * rest
-            g = growth * r
-            r = 1.0 / (near + 1.0)
-        else:
-            near = slip + rest
-            g = r
-            r = 1.0 / (near + decay)
-        rest = near * r
-        t = [x[c] + g * t[c] for c in range(2)]
-        w = g if w is None else g * w
-        held_f[m] = r
-        held_r[m] = slip
-        fore[m] = w
+    def early(in_sem, own_sem):
+        own = pltpu.make_async_copy(cell_h, table.at[me], own_sem)
+        own.start()
+        loads = {}
+        for i, (name, src, dst) in enumerate(
+            (
+                ("stretch", stretch_h, stretch),
+                ("height", height_h, height),
+                ("owner", owner_h, owner),
+                ("target", target_h, target),
+                ("face", face_h, face),
+                ("prof", prof_h, prof),
+                ("forc", forc_h, forc),
+                ("area", area_h, area),
+                ("live", live_h, live),
+                ("owner_s", owner_h.at[me], owner_s),
+                ("target_s", target_h.at[me], target_s),
+            )
+        ):
+            loads[name] = pltpu.make_async_copy(src, dst, in_sem.at[i])
+            loads[name].start()
+
+        pl.semaphore_wait(barrier, 1 + (doms - 2) * ((me + doms - 1) // doms))
+        own.wait()
+
+        @pl.when(me == 0)
+        def _():
+            cell_copy(0, relay, cell_send, relay_recv).start()
+
+        @pl.when(me == relay)
+        def _():
+            cell_copy(0, 1, relay_send, relay_recv).wait_recv()
+
+        @pl.when(me != 0)
+        def _():
+            for peer in peers:
+
+                @pl.when((me == relay) & (peer != 0))
+                def _():
+                    cell_copy(0, peer, relay_send, cell_recv).start()
+
+                cell_copy(me, peer, cell_send, cell_recv).start()
+
+        eye = lax.broadcasted_iota(jnp.int32, (blocks, blocks), 0) == lax.broadcasted_iota(
+            jnp.int32, (blocks, blocks), 1
+        )
+
+        def as_column(row):
+            spread = jnp.broadcast_to(row.astype(F32), (blocks, blocks))
+            return jnp.sum(jnp.where(eye, spread, 0.0), axis=1, keepdims=True)
+
+        depth = sub * half
+        tall_rows = sub * (half + 1)
+        row_id = lax.broadcasted_iota(jnp.int32, (tall_rows, depth), 0)
+        col_id = lax.broadcasted_iota(jnp.int32, (tall_rows, depth), 1)
+        shift = row_id // sub - col_id % half
+        same = row_id % sub == col_id // half
+        turn = jnp.where(
+            same, (shift == 0).astype(F32) - (shift == 1).astype(F32), 0.0
+        ).astype(BF16)
+
+        loads["stretch"].wait()
+        loads["height"].wait()
+        rate = BASE_RATE + as_column(stretch[...])
+        tall = height[...].astype(F32)
+        step_rate = jnp.broadcast_to(rate / points, wide)
+        growth = jnp.exp(step_rate)
+        decay = 1.0 / growth
+        first = (growth - 1.0) / (jnp.exp(jnp.broadcast_to(rate, wide)) - 1.0)
+        gap_scale = 0.5 * tall * first * (1.0 + growth)
+        base_scale = TIME_STEP * VISCOSITY / (first * tall * gap_scale)
+        quad_scale = TIME_STEP**0.5 * KARMAN / ((growth - 1.0) * gap_scale)
+        mid_first = 0.5 * (1.0 + growth)
+
+        def grid_levels(start, base_scale, quad_scale):
+            chunk = min(8, half)
+
+            def body(i, carry):
+                shrink, space = carry
+                for j in range(chunk):
+                    m = start + i * chunk + j
+                    base[m] = base_scale * (shrink * shrink)
+                    ratio = quad_scale * ((mid_first - shrink) * shrink)
+                    quad[m] = ratio * ratio
+                    gap[m] = space
+                    shrink = shrink * decay
+                    space = space * growth
+                return shrink, space
+
+            return lambda carry: lax.fori_loop(0, half // chunk, body, carry)
+
+        shrink, space = grid_levels(0, base_scale, quad_scale)((jnp.ones(wide, F32), gap_scale))
+        grid_levels(half, base_scale * growth, quad_scale * growth)((shrink, space * decay))
+
+        for name in ("owner", "target", "face"):
+            loads[name].wait()
+        face_now = face[...]
+        face_down = jnp.transpose(face_now.astype(F32))
+        cell_ids = lax.broadcasted_iota(jnp.int32, (faces, faces), 1).astype(F32)
+        for b in range(blocks):
+            pick[b // 2, pl.ds(b % 2 * faces, faces), :] = (
+                (cell_ids == face_down[:, b : b + 1]).astype(F32).astype(BF16)
+            )
+        own_row = owner[me]
+        aim_row = 2 * target[me]
+        terms = 4 * blocks
+        widen = (
+            lax.broadcasted_iota(jnp.int32, (blocks, terms), 1) // 4
+            == lax.broadcasted_iota(jnp.int32, (blocks, terms), 0)
+        ).astype(F32).astype(BF16)
+        own_wide = jnp.dot(own_row.astype(F32).astype(BF16), widen, preferred_element_type=F32)
+        aim_wide = jnp.dot(aim_row.astype(F32).astype(BF16), widen, preferred_element_type=F32)
+        comp = lax.broadcasted_iota(jnp.int32, (1, terms), 1) % 2
+        slot_of = (own_wide * rows + aim_wide).astype(jnp.int32) + comp
+        there = (
+            lax.broadcasted_iota(jnp.int32, (slots, terms), 0) == slot_of
+        ).astype(F32).astype(BF16)
+        place[...] = jnp.concatenate([there, there], axis=1)
+
+        loads["prof"].wait()
+        for i in range(blocks // sub):
+            group = pl.ds(i * sub, sub)
+            for c in range(2):
+                below = None
+                for part in range(2):
+                    levels = prof[group, c, pl.ds(part * half, half), :].reshape(depth, faces)
+                    steps = jnp.dot(turn, levels, preferred_element_type=F32)
+                    for j in range(half):
+                        m = part * half + j
+                        step = steps[sub * j : sub * (j + 1)]
+                        if j == 0 and part:
+                            step += below
+                        jump[m, c, group] = gap[m, group] * step
+                    below = steps[depth:tall_rows]
+                last[c, group] = below
+        for name in ("owner_s", "target_s"):
+            loads[name].wait()
+        for b in range(blocks):
+            row_at[b] = owner_s[0, b] * rows + 2 * target_s[0, b]
+            spot_at[b] = target_s[0, b] + rows * jnp.minimum(jnp.abs(owner_s[0, b] - peers[0]), 1)
+        loads["forc"].wait()
+        forc32[...] = forc[...].astype(F32)
+        loads["area"].wait()
+        loads["live"].wait()
+
+        slip = slip_of(0, speed((jump[0, 0], jump[0, 1])))
+        r = 1.0 / (slip + 1.0)
+        rest = slip * r
+        fore[0] = jnp.ones(wide, F32)
+        held_f[0] = r
+        held_r[0] = slip
+        t = [jump[0, 0], jump[0, 1]]
+        w = None
         for c in range(2):
-            held_t[m, c] = t[c]
-    last_rest = rest
-    y, push_part, top_part = None, None, None
-    for m in range(top_row - 1, -1, -1):
-        r, slip = held_f[m], held_r[m]
-        if y is None:
-            y = [r * held_t[m, c] for c in range(2)]
-            push_part = r * fore[m]
-            top_part = r * decay
-            brink, brink_push = y, push_part
-        else:
-            y = [r * (held_t[m, c] + (y[c] if m < half else decay * y[c])) for c in range(2)]
-            push_part = r * (fore[m] + (push_part if m < half else decay * push_part))
-            top_part = r * (top_part if m < half else decay * top_part)
+            held_t[0, c] = t[c]
+        for m in range(1, top_row):
+            x = (jump[m, 0], jump[m, 1])
+            slip = slip_of(m, speed(x))
+            if m < half:
+                near = slip + growth * rest
+                g = growth * r
+                r = 1.0 / (near + 1.0)
+            else:
+                near = slip + rest
+                g = r
+                r = 1.0 / (near + decay)
+            rest = near * r
+            t = [x[c] + g * t[c] for c in range(2)]
+            w = g if w is None else g * w
+            held_f[m] = r
+            held_r[m] = slip
+            fore[m] = w
+            for c in range(2):
+                held_t[m, c] = t[c]
+        last_rest = rest
+        y, push_part, top_part = None, None, None
+        for m in range(top_row - 1, -1, -1):
+            r, slip = held_f[m], held_r[m]
+            if y is None:
+                y = [r * held_t[m, c] for c in range(2)]
+                push_part = r * fore[m]
+                top_part = r * decay
+                brink, brink_push = y, push_part
+            else:
+                y = [r * (held_t[m, c] + (y[c] if m < half else decay * y[c])) for c in range(2)]
+                push_part = r * (fore[m] + (push_part if m < half else decay * push_part))
+                top_part = r * (top_part if m < half else decay * top_part)
+            for c in range(2):
+                jump[m, c] = slip * y[c]
+            by_push[m] = slip * push_part
+            by_top[m] = slip * top_part
+        edge[0] = last_rest
+        edge[1] = brink_push
         for c in range(2):
-            jump[m, c] = slip * y[c]
-        by_push[m] = slip * push_part
-        by_top[m] = slip * top_part
-    edge[0] = last_rest
-    edge[1] = brink_push
-    for c in range(2):
-        edge[2 + c] = brink[c]
+            edge[2 + c] = brink[c]
+        scale[0] = growth
+        scale[1] = decay
+
+    pl.run_scoped(
+        early, pltpu.SemaphoreType.DMA((11,)), pltpu.SemaphoreType.DMA(())
+    )
+    growth, decay = scale[0], scale[1]
+    face_now = face[...]
 
     @pl.when(me == relay)
     def _():
@@ -458,6 +469,27 @@
             [jnp.where(upper, both, 0.0), jnp.where(upper, 0.0, both)], axis=1
         ).astype(BF16)
         cells[pl.ds(8 * p, 8), :] = jnp.dot(pair, pick[p], preferred_element_type=F32)
+    spots = lax.broadcasted_iota(jnp.int32, (rows // 2, faces), 0)
+    sums = [jnp.zeros((rows // 2, faces), F32) for _ in range(2)]
+    for b in range(blocks):
+        here = spots == spot_at[b]
+        for c in range(2):
+            row = cells[pl.ds(4 * b + c, 1), :] + cells[pl.ds(4 * b + 2 + c, 1), :]
+            sums[c] += jnp.where(here, jnp.broadcast_to(row, (rows // 2, faces)), 0.0)
+    for c in range(2):
+        early_out[pl.ds(c, rows // 2, stride=2), :] = sums[c]
+
+    def force_copy(src, peer):
+        return pltpu.make_async_remote_copy(
+            src_ref=src,
+            dst_ref=arrived.at[lax.rem(peer - me + doms, doms) - 1],
+            send_sem=force_send,
+            recv_sem=force_recv,
+            device_id={"dom": peer},
+            device_id_type=MESH,
+        )
+
+    force_copy(early_out, peers[0]).start()
     by_cell = cells[...]
     top = by_cell.astype(BF16)
     low = (by_cell - top.astype(F32)).astype(BF16)
@@ -465,15 +497,8 @@
         place[...], jnp.concatenate([top, low], axis=0), preferred_element_type=F32
     )
     packed[...] = total.reshape(doms, rows, faces)
-    for peer in peers:
-        pltpu.make_async_remote_copy(
-            src_ref=packed.at[peer],
-            dst_ref=arrived.at[lax.rem(peer - me + doms, doms) - 1],
-            send_sem=force_send,
-            recv_sem=force_recv,
-            device_id={"dom": peer},
-            device_id_type=MESH,
-        ).start()
+    for peer in peers[1:]:
+        force_copy(packed.at[peer], peer).start()
     forces = pltpu.make_async_remote_copy(
         src_ref=packed.at[pl.ds(0, doms - 1)],
         dst_ref=arrived,
@@ -482,24 +507,24 @@
         device_id={"dom": relay},
         device_id_type=MESH,
     )
+    @pl.when(me == 0)
+    def _():
+        cells_of(1, cell_send, relay_recv).wait_send()
+
+    @pl.when(me != 0)
+    def _():
+        cells_of(doms - 1, cell_send, cell_recv).wait_send()
+
+    @pl.when(me == relay)
+    def _():
+        cells_of(doms - 2, relay_send, cell_recv).wait_send()
+
+    forces.wait_send()
     forces.wait_recv()
     result = packed[me]
     for j in range(doms - 1):
         result += arrived[j]
     force_ref[...] = result
-    forces.wait_send()
-
-    @pl.when(me == 0)
-    def _():
-        cells_of(1, cell_send, relay_recv).wait_send()
-
-    @pl.when(me != 0)
-    def _():
-        cells_of(doms - 1, cell_send, cell_recv).wait_send()
-
-    @pl.when(me == relay)
-    def _():
-        cells_of(doms - 2, relay_send, cell_recv).wait_send()
 
 
 def emit(shear_ref, force_ref, shear_out, force_out, sem):
@@ -571,19 +596,20 @@
             pltpu.VMEM((2, blocks, faces), F32),
             pltpu.VMEM((4, blocks, faces), F32),
             pltpu.VMEM((2, blocks, faces), F32),
+            pltpu.VMEM((2, blocks, faces), F32),
             pltpu.VMEM((doms * rows, faces), F32),
             pltpu.VMEM((2 * blocks, faces), F32),
             pltpu.SMEM((1, blocks), jnp.int32),
             pltpu.SMEM((1, blocks), jnp.int32),
             pltpu.SMEM((blocks,), jnp.int32),
+            pltpu.SMEM((blocks,), jnp.int32),
+            pltpu.VMEM((rows, faces), F32),
             pltpu.VMEM((blocks // 2, 2 * faces, faces), BF16),
             pltpu.VMEM((doms * rows, 8 * blocks), BF16),
             pltpu.VMEM((4 * blocks, faces), F32),
             pltpu.VMEM((doms, rows, faces), F32),
             pltpu.VMEM((doms - 1, rows, faces), F32),
             pltpu.VMEM((2 * blocks, faces), F32),
-            dma((len(args) + 1,)),
-            dma,
             dma,
             dma,
             dma,

time: 17.5 us -> 17.2 us (0.983)
  Pallas kernels: 16.7 us -> 16.5 us
    pallas_call x1, Pallas kernels: 16.1 us -> 15.8 us  [body(): pl.pallas_call(functools.partial(kernel, doms, grps), out_shape=(jax.Shap...]
where the time goes in v4:
time: 17.2 us; the launch traced here: 17.1 us
  Pallas kernels  16.5 us (96%)
  between operations  0.64 us (4%)
    pallas_call x1, Pallas kernels, body(): pl.pallas_call(functools.partial(kernel, doms, grps), out_shape=(jax.Shap...  15.8 us
    pallas_call x1, Pallas kernels, body(): pl.pallas_call(emit, out_shape=(jax.ShapeDtypeStruct(shear.shape, F32), j...  0.63 us

profile of v4, /device:TPU:0, one launch (start us, length us, event | category | flops | bytes accessed | tf_op | source)
XLA Modules:
  0.0 17.1 jit_solution(9378768087250213147)
XLA Ops:
  0.6 15.8 %wall_model.1 = (f32[48,128]{1,0:T(8,128)S(1)}, f32[24,128]{1,0:T(8,128)S(1)}) custom-call(bf16[24,2,64,128]{3,2,1,0:T(8,128)(2,1)} %prof_h.1, bf16[48,128]{1,0:T(8,128)(2,1)} %bitcast.6, bf16[24,128]{1,0:T(8,128)(2,1)} %height_h.1, f32[24,128]{1,0:T(8,128)} %area_h.1, s32[1,24]{1,0:T(1,128)} %bitcast.8, s32[24,128]{1,0:T(8,128)} %face_h.1, ...), custom_call_target="tpu_custom_call" | custom-call | tf_op jit(solution)/shard_map/wall_model/pallas_call | solution.py:574
  16.5 0.6 %emit.1 = (f32[48,128]{1,0:T(8,128)}, f32[24,128]{1,0:T(8,128)}) custom-call(f32[48,128]{1,0:T(8,128)S(1)} %get-tuple-element.6.shear_ref, f32[24,128]{1,0:T(8,128)S(1)} %get-tuple-element.7.force_ref), custom_call_target="tpu_custom_call" | custom-call | tf_op jit(solution)/shard_map/emit/pallas_call | solution.py:625

commit v5 on v4

--- a/solution.py
+++ b/solution.py
@@ -347,7 +347,7 @@
     def _():
         cells_of(doms - 1, cell_send, cell_recv).wait_recv()
 
-    held[...] = table[...].astype(F32).reshape(slots, faces)
+    held[pl.ds(0, slots), :] = table[...].astype(F32).reshape(slots, faces)
     for b in range(blocks):
         rows_of[pl.ds(2 * b, 2), :] = held[pl.ds(row_at[b], 2), :]
     edge_low, edge_high, x_top = [], [], []
@@ -489,8 +489,8 @@
             device_id_type=MESH,
         )
 
-    force_copy(early_out, peers[0]).start()
-    by_cell = cells[...]
+    force_copy(early_out.at[pl.ds(0, rows)], peers[0]).start()
+    by_cell = cells[pl.ds(0, 4 * blocks), :]
     top = by_cell.astype(BF16)
     low = (by_cell - top.astype(F32)).astype(BF16)
     total = jnp.dot(
@@ -597,16 +597,16 @@
             pltpu.VMEM((4, blocks, faces), F32),
             pltpu.VMEM((2, blocks, faces), F32),
             pltpu.VMEM((2, blocks, faces), F32),
-            pltpu.VMEM((doms * rows, faces), F32),
-            pltpu.VMEM((2 * blocks, faces), F32),
+            pltpu.VMEM((doms * rows + 8, faces), F32),
+            pltpu.VMEM((2 * blocks + 8, faces), F32),
             pltpu.SMEM((1, blocks), jnp.int32),
             pltpu.SMEM((1, blocks), jnp.int32),
             pltpu.SMEM((blocks,), jnp.int32),
             pltpu.SMEM((blocks,), jnp.int32),
-            pltpu.VMEM((rows, faces), F32),
+            pltpu.VMEM((rows + 16, faces), F32),
             pltpu.VMEM((blocks // 2, 2 * faces, faces), BF16),
             pltpu.VMEM((doms * rows, 8 * blocks), BF16),
-            pltpu.VMEM((4 * blocks, faces), F32),
+            pltpu.VMEM((4 * blocks + 8, faces), F32),
             pltpu.VMEM((doms, rows, faces), F32),
             pltpu.VMEM((doms - 1, rows, faces), F32),
             pltpu.VMEM((2 * blocks, faces), F32),

time: 17.2 us -> 17.2 us (level)
  no operation moved by 1% of the time
where the time goes in v5:
time: 17.2 us; the launch traced here: 17.1 us
  Pallas kernels  16.5 us (96%)
  between operations  0.64 us (4%)
    pallas_call x1, Pallas kernels, body(): pl.pallas_call(functools.partial(kernel, doms, grps), out_shape=(jax.Shap...  15.8 us
    pallas_call x1, Pallas kernels, body(): pl.pallas_call(emit, out_shape=(jax.ShapeDtypeStruct(shear.shape, F32), j...  0.63 us

profile of v5, /device:TPU:0, one launch (start us, length us, event | category | flops | bytes accessed | tf_op | source)
XLA Modules:
  0.0 17.1 jit_solution(14157138617378517864)
XLA Ops:
  0.6 15.8 %wall_model.1 = (f32[48,128]{1,0:T(8,128)S(1)}, f32[24,128]{1,0:T(8,128)S(1)}) custom-call(bf16[24,2,64,128]{3,2,1,0:T(8,128)(2,1)} %prof_h.1, bf16[48,128]{1,0:T(8,128)(2,1)} %bitcast.6, bf16[24,128]{1,0:T(8,128)(2,1)} %height_h.1, f32[24,128]{1,0:T(8,128)} %area_h.1, s32[1,24]{1,0:T(1,128)} %bitcast.8, s32[24,128]{1,0:T(8,128)} %face_h.1, ...), custom_call_target="tpu_custom_call" | custom-call | tf_op jit(solution)/shard_map/wall_model/pallas_call | solution.py:574
  16.5 0.6 %emit.1 = (f32[48,128]{1,0:T(8,128)}, f32[24,128]{1,0:T(8,128)}) custom-call(f32[48,128]{1,0:T(8,128)S(1)} %get-tuple-element.6.shear_ref, f32[24,128]{1,0:T(8,128)S(1)} %get-tuple-element.7.force_ref), custom_call_target="tpu_custom_call" | custom-call | tf_op jit(solution)/shard_map/emit/pallas_call | solution.py:625

commit v6 on v5

--- a/solution.py
+++ b/solution.py
@@ -107,6 +107,7 @@
             pl.semaphore_signal(barrier, inc=1, device_id={"dom": peer}, device_id_type=MESH)
 
     peers = [peer_at(k) for k in range(doms - 1)]
+    lands = [lax.rem(peer - me + doms, doms) - 1 for peer in peers]
 
     def cell_copy(slot, peer, send, recv):
         return pltpu.make_async_remote_copy(
@@ -479,17 +480,17 @@
     for c in range(2):
         early_out[pl.ds(c, rows // 2, stride=2), :] = sums[c]
 
-    def force_copy(src, peer):
+    def force_copy(src, land, peer):
         return pltpu.make_async_remote_copy(
             src_ref=src,
-            dst_ref=arrived.at[lax.rem(peer - me + doms, doms) - 1],
+            dst_ref=arrived.at[land],
             send_sem=force_send,
             recv_sem=force_recv,
             device_id={"dom": peer},
             device_id_type=MESH,
         )
 
-    force_copy(early_out.at[pl.ds(0, rows)], peers[0]).start()
+    force_copy(early_out.at[pl.ds(0, rows)], lands[0], peers[0]).start()
     by_cell = cells[pl.ds(0, 4 * blocks), :]
     top = by_cell.astype(BF16)
     low = (by_cell - top.astype(F32)).astype(BF16)
@@ -497,8 +498,8 @@
         place[...], jnp.concatenate([top, low], axis=0), preferred_element_type=F32
     )
     packed[...] = total.reshape(doms, rows, faces)
-    for peer in peers[1:]:
-        force_copy(packed.at[peer], peer).start()
+    for land, peer in zip(lands[1:], peers[1:]):
+        force_copy(packed.at[peer], land, peer).start()
     forces = pltpu.make_async_remote_copy(
         src_ref=packed.at[pl.ds(0, doms - 1)],
         dst_ref=arrived,
@@ -527,15 +528,18 @@
     force_ref[...] = result
 
 
-def emit(shear_ref, force_ref, shear_out, force_out, sem):
-    copies = (
-        pltpu.make_async_copy(shear_ref, shear_out, sem.at[0]),
-        pltpu.make_async_copy(force_ref, force_out, sem.at[1]),
-    )
-    for copy in copies:
-        copy.start()
-    for copy in copies:
-        copy.wait()
+def emit(shear_ref, force_ref, shear_out, force_out):
+    def run(sem):
+        copies = (
+            pltpu.make_async_copy(force_ref, force_out, sem.at[0]),
+            pltpu.make_async_copy(shear_ref, shear_out, sem.at[1]),
+        )
+        for copy in copies:
+            copy.start()
+        for copy in copies:
+            copy.wait()
+
+    pl.run_scoped(run, pltpu.SemaphoreType.DMA((2,)))
 
 
 def body(
@@ -630,7 +634,6 @@
         ),
         in_specs=[pl.BlockSpec(memory_space=pl.ANY)] * 2,
         out_specs=(pl.BlockSpec(memory_space=pl.ANY),) * 2,
-        scratch_shapes=[dma((2,))],
         compiler_params=pltpu.CompilerParams(vmem_limit_bytes=1 << 20),
         name="emit",
     )(shear, force)

time: 17.2 us -> 17.2 us (level)
  no operation moved by 1% of the time
where the time goes in v6:
time: 17.2 us; the launch traced here: 17.1 us
  Pallas kernels  16.4 us (95%)
  between operations  0.64 us (4%)
    pallas_call x1, Pallas kernels, body(): pl.pallas_call(functools.partial(kernel, doms, grps), out_shape=(jax.Shap...  15.8 us
    pallas_call x1, Pallas kernels, body(): pl.pallas_call(emit, out_shape=(jax.ShapeDtypeStruct(shear.shape, F32), j...  0.61 us

profile of v6, /device:TPU:0, one launch (start us, length us, event | category | flops | bytes accessed | tf_op | source)
XLA Modules:
  0.0 17.1 jit_solution(8804939452057073285)
XLA Ops:
  0.6 15.8 %wall_model.1 = (f32[48,128]{1,0:T(8,128)S(1)}, f32[24,128]{1,0:T(8,128)S(1)}) custom-call(bf16[24,2,64,128]{3,2,1,0:T(8,128)(2,1)} %prof_h.1, bf16[48,128]{1,0:T(8,128)(2,1)} %bitcast.6, bf16[24,128]{1,0:T(8,128)(2,1)} %height_h.1, f32[24,128]{1,0:T(8,128)} %area_h.1, s32[1,24]{1,0:T(1,128)} %bitcast.8, s32[24,128]{1,0:T(8,128)} %face_h.1, ...), custom_call_target="tpu_custom_call" | custom-call | tf_op jit(solution)/shard_map/wall_model/pallas_call | solution.py:578
  16.5 0.6 %emit.1 = (f32[48,128]{1,0:T(8,128)}, f32[24,128]{1,0:T(8,128)}) custom-call(f32[48,128]{1,0:T(8,128)S(1)} %get-tuple-element.6.shear_ref, f32[24,128]{1,0:T(8,128)S(1)} %get-tuple-element.7.force_ref), custom_call_target="tpu_custom_call" | custom-call | tf_op jit(solution)/shard_map/emit/pallas_call | solution.py:629
